TPU v7x, 32 devices: a whole 2x2x4 slice. The times are simulated.
32 devices in a mesh: row: 8 (over y, x, core), col: 4 (over z).
Axes of the slice: x: 2, y: 2, z: 4, core: 2. Of those that a mesh axis runs over, the one named last changes fastest.
Arguments:
- a_blocks: bfloat16 [1024, 16, 128, 128], P(('row', 'col')), may hold values from -0.0625 to 0.0625
- omega: bfloat16 [16384, 256], P('col'), may hold values from -6 to 6
- route_dest: int32 [1024, 1], P(('row', 'col')), may hold values from 0 to 7; in each aligned block of 32 rows (0 to 31, 32 to 63, ...) at most 4 rows name the same one
- row_target: int32 [1024], P(('row', 'col')), may hold values from 0 to 31
- col_target: int32 [1024, 16], P(('row', 'col')), may hold values from 0 to 31
Outputs:
- basis: float32 [32768, 256], P(('row', 'col'))
- factor: float32 [256, 256], replicated
Inputs may be any that keep to these rules, and one draw needn't show every extreme that they name: `route_dest`: among the 32 rows of one device no value appears more than 4 times, and in some device's rows one value appears exactly 4 times.
All inputs are finite; a program needn't handle non-finite values.
Results may differ from a plain program's by a relative error of at most 0.003.
Values may be sent and summed in bfloat16 or wider, within the bound.
A program may use at most 192 MiB of HBM per device.

v0:
```python
import jax
import jax.numpy as jnp
from jax import lax
from jax.sharding import PartitionSpec as P

RB_DEV = 8
CAP = 4


def product(left, right):
    return jnp.dot(left, right, precision=lax.Precision.HIGHEST, preferred_element_type=jnp.float32)


def upper_factor(gram):
    order = gram.shape[0]
    lower = jnp.linalg.cholesky(gram)
    identity = jnp.eye(order, dtype=jnp.float32)
    inverse = jax.scipy.linalg.solve_triangular(lower, identity, lower=True)
    return (lower.T, inverse.T)


def body(a_blocks, omega, route_dest, row_target, col_target):
    targets_here, group_size, block_order, _ = a_blocks.shape
    sketch_width = omega.shape[1]
    row_count = lax.axis_size("row")
    slab = omega.reshape(omega.shape[0] // block_order, block_order, sketch_width)
    picked = slab[col_target]
    partial_value = jnp.einsum(
        "tgij,tgjk->tik", a_blocks, picked, preferred_element_type=jnp.float32
    ).astype(jnp.bfloat16)
    destination = route_dest[:, 0]
    positions = jnp.arange(targets_here, dtype=jnp.int32)
    same_owner = destination[:, None] == destination[None, :]
    earlier = positions[None, :] < positions[:, None]
    rank = jnp.sum(jnp.logical_and(same_owner, earlier), axis=1)
    slot_of = destination * CAP + rank
    slot_ids = jnp.arange(row_count * CAP, dtype=jnp.int32)
    matches = slot_of[None, :] == slot_ids[:, None]
    filled = jnp.any(matches, axis=1)
    source = jnp.sum(jnp.where(matches, positions[None, :], 0), axis=1)
    send_values = jnp.where(
        filled[:, None, None], partial_value[source], jnp.zeros((), jnp.bfloat16)
    )
    send_values = send_values.reshape(row_count, CAP, block_order, sketch_width)
    send_rows = jnp.where(filled, row_target[source], -1).reshape(row_count, CAP)
    got_values, got_rows = (
        lax.all_to_all(send_values, "row", split_axis=0, concat_axis=0, tiled=True),
        lax.all_to_all(send_rows, "row", split_axis=0, concat_axis=0, tiled=True),
    )
    flat_values = got_values.reshape(row_count * CAP, block_order, sketch_width)
    flat_rows = got_rows.reshape(row_count * CAP)
    count = lax.axis_size("col") * (RB_DEV * block_order)
    block_total = count // block_order
    wanted = jnp.arange(block_total, dtype=jnp.int32)
    selector = (flat_rows[None, :] == wanted[:, None]).astype(jnp.bfloat16)
    term = jnp.einsum("bs,sik->bik", selector, flat_values, preferred_element_type=jnp.float32)
    sketch = lax.psum_scatter(
        term.reshape(count, sketch_width), "col", scatter_dimension=0, tiled=True
    )
    gram_one = lax.psum(product(sketch.T, sketch), ("row", "col"))
    first, first_inv = upper_factor(gram_one)
    once = product(sketch, first_inv)
    gram_two = lax.psum(product(once.T, once), ("row", "col"))
    second, second_inv = upper_factor(gram_two)
    basis = product(once, second_inv)
    factor = product(second, first)
    total_rows = float(sketch.shape[0] * lax.axis_size(("row", "col")))
    scale_root = jnp.sqrt(jnp.float32(total_rows))
    return (basis * scale_root, factor / scale_root)


def solution(mesh):
    return jax.shard_map(
        body,
        mesh=mesh,
        in_specs=(
            P(("row", "col"), None, None, None),
            P("col", None),
            P(("row", "col"), None),
            P(("row", "col")),
            P(("row", "col"), None),
        ),
        out_specs=(P(("row", "col"), None), P()),
        check_vma=False,
    )
```

profile of v0, /device:TPU:0, one launch (start us, length us, event | category | flops | bytes accessed | tf_op | source)
XLA Modules:
  0.0 577.7 jit_solution(14751288368338231780)
XLA Ops:
  7.2 1.0 convert_reduce_fusion
  8.2 0.7 multiply_add_fusion
  9.1 1.4 gather_fusion
  10.5 0.7 select_n.44
  11.1 5.2 all-to-all-start
  16.4 0.7 compare_select_fusion
  17.3 16.1 %gather_fusion.1 = bf16[512,128,256]{2,1,0:T(8,128)(2,1)} fusion(bf16[32,128,256]{2,1,0:T(8,128)(2,1)S(1)} %bitcast.94, s32[1024]{0:T(1024)S(1)} %pad_clamp_fusion), kind=kCustom, calls=%fused_computation.1 | custom fusion | bytes 67110912 | tf_op jit(solution)/shard_map/gather | solution.py:27
  33.4 19.5 %fusion = bf16[32,128,256]{1,2,0:T(8,128)(2,1)} fusion(bf16[32,16,128,256]{3,2,1,0:T(8,128)(2,1)} %bitcast.95, bf16[32,16,128,128]{3,2,1,0:T(8,128)(2,1)} %param.8), kind=kOutput, calls=%fused_computation.9 | convolution fusion | flops 4296015872 | bytes 52428800 | tf_op jit(solution)/shard_map/tgij,tgjk->tik/dot_general | solution.py:28
  52.9 2.5 gather_fusion.2
  55.5 1.6 broadcast_select_fusion
  57.0 4.2 all-to-all-start.1
  61.2 0.5 broadcast.141
  61.7 0.7 reduce.11
  62.5 25.3 %all-to-all-done.1 = bf16[8,4,128,256]{2,3,1,0:T(8,128)(2,1)S(1)} async-done(((bf16[8,4,128,256]{2,3,1,0:T(8,128)(2,1)}), bf16[8,4,128,256]{2,3,1,0:T(8,128)(2,1)S(1)}, u32[]{:S(2)}, u32[]{:S(2)}) %all-to-all-start.1) | async-done | bytes 2097184 | tf_op jit(solution)/shard_map/all_to_all | solution.py:47
  87.8 1.3 copy-done.3
  89.2 3.4 copy.42
  92.6 0.7 fusion.36
  93.3 4.4 copy.34
  97.7 76.3 %reduce-scatter.2.cloned.1.call-done = f32[1024,256]{1,0:T(8,128)} async-done(((f32[4096,256]{1,0:T(8,128)}), f32[1024,256]{1,0:T(8,128)}) %reduce-scatter.2.cloned.1.call-update) | async-done | bytes 1048592 | tf_op jit(solution)/shard_map/reduce_scatter | solution.py:57
  174.0 4.1 fusion.46
  178.1 0.5 all-reduce.6.cloned.1.call-start
  178.6 128.6 %all-reduce.4.cloned.1.call-done = f32[256,256]{0,1:T(8,128)} async-done(((f32[256,256]{0,1:T(8,128)}), f32[256,256]{0,1:T(8,128)}) %all-reduce.4.cloned.1.call-update) | async-done | bytes 262160 | tf_op jit(solution)/shard_map/psum | solution.py:60
  307.2 1.1 copy.36
  308.3 1.0 fusion.9
  309.3 11.7 %cholesky.130 = f32[128,128]{1,0:T(8,128)S(1)} custom-call(f32[128,128]{1,0:T(8,128)S(1)} %cholesky.194), custom_call_target="Cholesky" | custom-call | tf_op jit(solution)/shard_map/jit(cholesky)/cholesky | solution.py:16
  321.1 9.8 %custom-call.13 = f32[1,128,128]{1,2,0:T(8,128)S(1)} custom-call(f32[1,128,128]{2,1,0:T(8,128)S(1)} %get-tuple-element.47), custom_call_target="InvertDiagBlocksLowerTriangular" | custom-call | tf_op jit(solution)/shard_map/jit(cholesky)/cholesky | solution.py:16
  330.9 0.2 constant_dynamic-update-slice_fusion.3
  331.1 0.3 convolution_subtract_fusion.3
  331.4 11.7 %cholesky.147 = f32[128,128]{1,0:T(8,128)S(1)} custom-call(f32[128,128]{1,0:T(8,128)S(1)} %convolution_subtract_fusion.3), custom_call_target="Cholesky" | custom-call | tf_op jit(solution)/shard_map/jit(cholesky)/cholesky | solution.py:16
  343.1 0.7 compare_reduce_fusion.2
  345.3 4.1 while.4
  345.3 0.6 fusion.67
  345.9 1.4 bitcast_dynamic-update-slice_fusion.4
  347.4 0.6 fusion.67
  348.0 1.4 bitcast_dynamic-update-slice_fusion.4
  349.4 19.8 %custom-call.14 = f32[2,128,128]{1,2,0:T(8,128)S(1)} custom-call(f32[2,128,128]{2,1,0:T(8,128)S(1)} %get-tuple-element.18), custom_call_target="InvertDiagBlocksLowerTriangular" | custom-call | tf_op jit(solution)/shard_map/jit(_solve_triangular)/triangular_solve | solution.py:18
  369.3 0.3 fusion.21
  369.6 0.3 convolution_subtract_fusion.1
  369.9 0.3 fusion.28
  370.2 1.0 fusion.1
  371.2 2.5 fusion.47
  373.8 125.9 %all-reduce.6.cloned.1.call-done = f32[256,256]{0,1:T(8,128)} async-done(((f32[256,256]{0,1:T(8,128)}), f32[256,256]{0,1:T(8,128)}) %all-reduce.6.cloned.1.call-update) | async-done | bytes 262160 | tf_op jit(solution)/shard_map/psum | solution.py:63
  499.6 1.1 copy.38
  500.7 1.0 fusion.8
  501.7 11.7 %cholesky.164 = f32[128,128]{1,0:T(8,128)S(1)} custom-call(f32[128,128]{1,0:T(8,128)S(1)} %cholesky.197), custom_call_target="Cholesky" | custom-call | tf_op jit(solution)/shard_map/jit(cholesky)/cholesky | solution.py:16
  513.5 9.8 %custom-call.15 = f32[1,128,128]{1,2,0:T(8,128)S(1)} custom-call(f32[1,128,128]{2,1,0:T(8,128)S(1)} %get-tuple-element.43), custom_call_target="InvertDiagBlocksLowerTriangular" | custom-call | tf_op jit(solution)/shard_map/jit(cholesky)/cholesky | solution.py:16
  523.3 0.2 constant_dynamic-update-slice_fusion.1
  523.5 0.3 convolution_subtract_fusion.2
  523.8 11.9 %cholesky.181 = f32[128,128]{1,0:T(8,128)S(1)} custom-call(f32[128,128]{1,0:T(8,128)S(1)} %convolution_subtract_fusion.2), custom_call_target="Cholesky" | custom-call | tf_op jit(solution)/shard_map/jit(cholesky)/cholesky | solution.py:16
  535.7 0.6 compare_reduce_fusion.1
  536.3 0.6 compare_reduce_fusion
  538.3 0.7 fusion.10
  539.0 1.2 convolution_multiply_fusion.1
  540.2 5.8 %while.5 = (s32[]{:T(128)}, f32[256,256]{1,0:T(8,128)}, s32[2,2]{1,0:T(2,128)S(1)}, f32[2,128,128]{2,1,0:T(8,128)S(1)}, s32[]{:T(128)}) while((s32[]{:T(128)}, f32[256,256]{1,0:T(8,128)}, s32[2,2]{1,0:T(2,128)S(1)}, f32[2,128,128]{2,1,0:T(8,128)S(1)}, s32[]{:T(128)}) %tuple.59), condition=%wide.while_cond.clone, body=%wide.while_body.clone.sunk | while | flops 2 | bytes 131189 | solution.py:18
  540.3 0.7 fusion.68
  540.9 2.2 bitcast_dynamic-update-slice_fusion.5
  543.2 0.7 fusion.68
  543.9 2.2 bitcast_dynamic-update-slice_fusion.5
  546.1 0.6 copy-done.4
  546.7 20.5 %custom-call.16 = f32[2,128,128]{1,2,0:T(8,128)S(1)} custom-call(f32[2,128,128]{2,1,0:T(8,128)} %copy-done.4), custom_call_target="InvertDiagBlocksLowerTriangular" | custom-call | tf_op jit(solution)/shard_map/jit(_solve_triangular)/triangular_solve | solution.py:18
  567.2 0.3 fusion.19
  567.5 1.1 convolution_subtract_fusion
  568.6 0.3 fusion.24
  569.0 2.0 convolution_multiply_fusion
  (42 shorter events, 1.1 us)
Async XLA Ops:
  7.2 10.1 %copy-start = (bf16[4096,256]{1,0:T(8,128)(2,1)S(1)}, bf16[4096,256]{1,0:T(8,128)(2,1)}, u32[]{:S(2)}) copy-start(bf16[4096,256]{1,0:T(8,128)(2,1)} %param.9) | copy-start | bytes 6291460
  11.1 45.9 %all-to-all-start = ((s32[8,1,4]{2,1,0:T(1,128)}), s32[8,1,4]{2,1,0:T(1,128)S(1)}, u32[]{:S(2)}, u32[]{:S(2)}) async-start(s32[8,1,4]{2,1,0:T(1,128)} %bitcast.3), calls=%async_computation | async-start | bytes 8192 | tf_op jit(solution)/shard_map/all_to_all | solution.py:48
  57.0 30.8 %all-to-all-start.1 = ((bf16[8,4,128,256]{2,3,1,0:T(8,128)(2,1)}), bf16[8,4,128,256]{2,3,1,0:T(8,128)(2,1)S(1)}, u32[]{:S(2)}, u32[]{:S(2)}) async-start(bf16[8,4,128,256]{2,3,1,0:T(8,128)(2,1)} %broadcast_select_fusion), calls=%async_computation.1 | async-start | bytes 4194304 | tf_op jit(solution)/shard_map/all_to_all | solution.py:47
  61.2 112.8 %reduce-scatter.2.cloned.1.call-start = ((), (), s32[]{:S(2)}) async-start(), calls=%async_computation.3 | async-start | bytes 5242880 | tf_op jit(solution)/shard_map/reduce_scatter | solution.py:57
  87.8 1.4 copy-start.3
  97.6 209.6 %all-reduce.4.cloned.1.call-start = ((), (), s32[]{:S(2)}) async-start(), calls=%async_computation.4 | async-start | bytes 524288 | tf_op jit(solution)/shard_map/psum | solution.py:60
  178.1 321.6 %all-reduce.6.cloned.1.call-start = ((), (), s32[]{:S(2)}) async-start(), calls=%async_computation.5 | async-start | bytes 524288 | tf_op jit(solution)/shard_map/psum | solution.py:63
  309.3 60.9 %copy-start.2 = (f32[1024,256]{1,0:T(8,128)S(1)}, f32[1024,256]{1,0:T(8,128)}, u32[]{:S(2)}) copy-start(f32[1024,256]{1,0:T(8,128)} %reduce-scatter.2.cloned.1.call-done) | copy-start | bytes 3145732
  540.2 30.7 %copy-start.1 = (bf16[4096,256]{1,0:T(8,128)(2,1)S(1)}, bf16[4096,256]{1,0:T(8,128)(2,1)}, u32[]{:S(2)}) copy-start(bf16[4096,256]{1,0:T(8,128)(2,1)} %param.9) | copy-start | bytes 6291460
  546.1 0.6 copy-start.4
Sparse Core Ops, SparseCore 0:
  97.8 76.1 reduce-scatter.1
  180.1 127.0 all-reduce.3
  373.9 125.6 all-reduce.5
where the time goes:
time: 586 us; the launch traced here: 578 us
  waiting for transfers between devices  356 us (61%)
  other arithmetic  117 us (20%)
  local copies, waits for them, and re-layouts  43.4 us (7%)
  matrix products  34.5 us (6%)
  between operations  16.9 us (3%)
  starting transfers between devices  9.95 us (2%)
    psum x1, waiting for transfers between devices, body(): gram_one = lax.psum(product(sketch.T, sketch), ('row', 'col'))  129 us
    psum x1, waiting for transfers between devices, body(): gram_two = lax.psum(product(once.T, once), ('row', 'col'))  126 us
    reduce_scatter x1, waiting for transfers between devices, body(): lax.psum_scatter(term.reshape(count, sketch_width), 'col', scatter_dimens...  76.3 us
    another operation x13, other arithmetic, upper_factor(): lower = jnp.linalg.cholesky(gram)  68.8 us
    another operation x5, other arithmetic, upper_factor(): inverse = jax.scipy.linalg.solve_triangular(lower, identity, lower=True)  41.1 us
    all_to_all x1, waiting for transfers between devices, body(): lax.all_to_all(send_values, 'row', split_axis=0, concat_axis=0, tiled=True)  25.3 us
    dot_general x1, matrix products, body(): jnp.einsum('tgij,tgjk->tik', a_blocks, picked, preferred_element_type=jnp...  19.5 us
    gather x1, local copies, waits for them, and re-layouts, body(): picked = slab[col_target]  16.1 us
  transfers between devices with their start and end apart: 5, of which 4 were waited for; matrix products, arithmetic and copies ran while one was open for 7% of the time, Pallas kernels for 0%

commit v1 on v0

--- a/solution.py
+++ b/solution.py
@@ -60,7 +60,7 @@
     gram_one = lax.psum(product(sketch.T, sketch), ("row", "col"))
     first, first_inv = upper_factor(gram_one)
     once = product(sketch, first_inv)
-    gram_two = lax.psum(product(once.T, once), ("row", "col"))
+    gram_two = jnp.sum(lax.all_gather(product(once.T, once), ("row", "col")), axis=0)
     second, second_inv = upper_factor(gram_two)
     basis = product(once, second_inv)
     factor = product(second, first)

time: 586 us -> 539 us (0.920)
  waiting for transfers between devices: 356 us -> 307 us
    psum x1 -> x0, waiting for transfers between devices: 126 us -> none  [body(): gram_two = lax.psum(product(once.T, once), ('row', 'col'))]
    all_gather x0 -> x1, waiting for transfers between devices: none -> 76.3 us  [body(): lax.all_gather(product(once.T, once), ('row', 'col'))]
  transfers between devices with their start and end apart: 5 -> 5, of which waited for: 4 -> 4; matrix products, arithmetic and copies ran while one was open for 7% -> 8% of each run, Pallas kernels for 0% -> 0%
where the time goes in v1:
time: 539 us; the launch traced here: 530 us
  waiting for transfers between devices  307 us (57%)
  other arithmetic  120 us (22%)
  local copies, waits for them, and re-layouts  42.3 us (8%)
  matrix products  34.5 us (6%)
  between operations  16.9 us (3%)
  starting transfers between devices  9.95 us (2%)
    psum x1, waiting for transfers between devices, body(): gram_one = lax.psum(product(sketch.T, sketch), ('row', 'col'))  129 us
    all_gather x1, waiting for transfers between devices, body(): lax.all_gather(product(once.T, once), ('row', 'col'))  76.3 us
    reduce_scatter x1, waiting for transfers between devices, body(): lax.psum_scatter(term.reshape(count, sketch_width), 'col', scatter_dimens...  76.3 us
    another operation x13, other arithmetic, upper_factor(): lower = jnp.linalg.cholesky(gram)  68.7 us
    another operation x5, other arithmetic, upper_factor(): inverse = jax.scipy.linalg.solve_triangular(lower, identity, lower=True)  41.1 us
    all_to_all x1, waiting for transfers between devices, body(): lax.all_to_all(send_values, 'row', split_axis=0, concat_axis=0, tiled=True)  25.3 us
    dot_general x1, matrix products, body(): jnp.einsum('tgij,tgjk->tik', a_blocks, picked, preferred_element_type=jnp...  19.5 us
    gather x1, local copies, waits for them, and re-layouts, body(): picked = slab[col_target]  16.1 us
  transfers between devices with their start and end apart: 5, of which 4 were waited for; matrix products, arithmetic and copies ran while one was open for 8% of the time, Pallas kernels for 0%

profile of v1, /device:TPU:0, one launch (start us, length us, event | category | flops | bytes accessed | tf_op | source)
XLA Modules:
  0.0 529.9 jit_solution(11958883564550688862)
XLA Ops:
  7.2 1.0 convert_reduce_fusion
  8.2 0.7 multiply_add_fusion
  9.1 1.4 gather_fusion
  10.5 0.7 select_n.44
  11.1 5.2 all-to-all-start
  16.4 0.7 compare_select_fusion
  17.3 16.1 %gather_fusion.1 = bf16[512,128,256]{2,1,0:T(8,128)(2,1)} fusion(bf16[32,128,256]{2,1,0:T(8,128)(2,1)S(1)} %bitcast.95, s32[1024]{0:T(1024)S(1)} %pad_clamp_fusion), kind=kCustom, calls=%fused_computation.1 | custom fusion | bytes 67110912 | tf_op jit(solution)/shard_map/gather | solution.py:27
  33.4 19.5 %fusion = bf16[32,128,256]{1,2,0:T(8,128)(2,1)} fusion(bf16[32,16,128,256]{3,2,1,0:T(8,128)(2,1)} %bitcast.96, bf16[32,16,128,128]{3,2,1,0:T(8,128)(2,1)} %param.8), kind=kOutput, calls=%fused_computation.9 | convolution fusion | flops 4296015872 | bytes 52428800 | tf_op jit(solution)/shard_map/tgij,tgjk->tik/dot_general | solution.py:28
  52.9 2.5 gather_fusion.2
  55.5 1.6 broadcast_select_fusion
  57.0 4.2 all-to-all-start.1
  61.2 0.5 broadcast.141
  61.7 0.7 reduce.11
  62.5 25.3 %all-to-all-done.1 = bf16[8,4,128,256]{2,3,1,0:T(8,128)(2,1)S(1)} async-done(((bf16[8,4,128,256]{2,3,1,0:T(8,128)(2,1)}), bf16[8,4,128,256]{2,3,1,0:T(8,128)(2,1)S(1)}, u32[]{:S(2)}, u32[]{:S(2)}) %all-to-all-start.1) | async-done | bytes 2097184 | tf_op jit(solution)/shard_map/all_to_all | solution.py:47
  87.8 1.3 copy-done.3
  89.2 3.4 copy.37
  92.6 0.7 fusion.36
  93.3 4.4 copy.31
  97.7 76.3 %reduce-scatter.2.cloned.1.call-done = f32[1024,256]{1,0:T(8,128)} async-done(((f32[4096,256]{1,0:T(8,128)}), f32[1024,256]{1,0:T(8,128)}) %reduce-scatter.2.cloned.1.call-update) | async-done | bytes 1048592 | tf_op jit(solution)/shard_map/reduce_scatter | solution.py:57
  174.0 4.1 fusion.46
  178.1 0.5 all-gather.3.cloned.1.call-start
  178.6 128.6 %all-reduce.3.cloned.1.call-done = f32[256,256]{0,1:T(8,128)} async-done(((f32[256,256]{0,1:T(8,128)}), f32[256,256]{0,1:T(8,128)}) %all-reduce.3.cloned.1.call-update) | async-done | bytes 262160 | tf_op jit(solution)/shard_map/psum | solution.py:60
  307.2 1.1 copy.33
  308.3 1.0 fusion.9
  309.3 11.7 %cholesky.130 = f32[128,128]{1,0:T(8,128)S(1)} custom-call(f32[128,128]{1,0:T(8,128)S(1)} %cholesky.194), custom_call_target="Cholesky" | custom-call | tf_op jit(solution)/shard_map/jit(cholesky)/cholesky | solution.py:16
  321.1 9.8 %custom-call.13 = f32[1,128,128]{1,2,0:T(8,128)S(1)} custom-call(f32[1,128,128]{2,1,0:T(8,128)S(1)} %get-tuple-element.47), custom_call_target="InvertDiagBlocksLowerTriangular" | custom-call | tf_op jit(solution)/shard_map/jit(cholesky)/cholesky | solution.py:16
  330.9 0.2 constant_dynamic-update-slice_fusion.3
  331.1 0.3 convolution_subtract_fusion.3
  331.4 11.7 %cholesky.147 = f32[128,128]{1,0:T(8,128)S(1)} custom-call(f32[128,128]{1,0:T(8,128)S(1)} %convolution_subtract_fusion.3), custom_call_target="Cholesky" | custom-call | tf_op jit(solution)/shard_map/jit(cholesky)/cholesky | solution.py:16
  343.1 0.7 compare_reduce_fusion.2
  345.2 4.0 while.4
  345.2 0.6 fusion.67
  345.8 1.4 bitcast_dynamic-update-slice_fusion.4
  347.2 0.6 fusion.67
  347.8 1.4 bitcast_dynamic-update-slice_fusion.4
  349.2 19.8 %custom-call.14 = f32[2,128,128]{1,2,0:T(8,128)S(1)} custom-call(f32[2,128,128]{2,1,0:T(8,128)S(1)} %get-tuple-element.18), custom_call_target="InvertDiagBlocksLowerTriangular" | custom-call | tf_op jit(solution)/shard_map/jit(_solve_triangular)/triangular_solve | solution.py:18
  369.0 0.3 fusion.21
  369.3 0.3 convolution_subtract_fusion.1
  369.6 0.3 fusion.28
  369.9 1.0 fusion.1
  371.0 2.5 fusion.47
  373.5 76.3 %all-gather.3.cloned.1.call-done = f32[8192,256]{1,0:T(8,128)} async-done(((f32[256,256]{1,0:T(8,128)}), f32[8192,256]{1,0:T(8,128)}) %all-gather.3.cloned.1.call-update) | async-done | bytes 8388624 | tf_op jit(solution)/shard_map/all_gather | solution.py:63
  449.8 3.9 reduce_sum.32
  453.8 0.1 copy.34
  453.9 11.7 %cholesky.164 = f32[128,128]{1,0:T(8,128)S(1)} custom-call(f32[128,128]{1,0:T(8,128)S(1)} %cholesky.197), custom_call_target="Cholesky" | custom-call | tf_op jit(solution)/shard_map/jit(cholesky)/cholesky | solution.py:16
  465.7 9.8 %custom-call.15 = f32[1,128,128]{1,2,0:T(8,128)S(1)} custom-call(f32[1,128,128]{2,1,0:T(8,128)S(1)} %get-tuple-element.43), custom_call_target="InvertDiagBlocksLowerTriangular" | custom-call | tf_op jit(solution)/shard_map/jit(cholesky)/cholesky | solution.py:16
  475.5 0.2 constant_dynamic-update-slice_fusion.1
  475.7 0.3 convolution_subtract_fusion.2
  476.0 11.9 %cholesky.181 = f32[128,128]{1,0:T(8,128)S(1)} custom-call(f32[128,128]{1,0:T(8,128)S(1)} %convolution_subtract_fusion.2), custom_call_target="Cholesky" | custom-call | tf_op jit(solution)/shard_map/jit(cholesky)/cholesky | solution.py:16
  487.9 0.6 compare_reduce_fusion.1
  488.6 0.6 compare_reduce_fusion
  490.5 0.7 fusion.10
  491.3 1.2 convolution_multiply_fusion.1
  492.5 5.8 %while.5 = (s32[]{:T(128)}, f32[256,256]{1,0:T(8,128)}, s32[2,2]{1,0:T(2,128)S(1)}, f32[2,128,128]{2,1,0:T(8,128)S(1)}, s32[]{:T(128)}) while((s32[]{:T(128)}, f32[256,256]{1,0:T(8,128)}, s32[2,2]{1,0:T(2,128)S(1)}, f32[2,128,128]{2,1,0:T(8,128)S(1)}, s32[]{:T(128)}) %tuple.59), condition=%wide.while_cond.clone, body=%wide.while_body.clone.sunk | while | flops 2 | bytes 131189 | solution.py:18
  492.5 0.7 fusion.68
  493.2 2.2 bitcast_dynamic-update-slice_fusion.5
  495.5 0.7 fusion.68
  496.1 2.2 bitcast_dynamic-update-slice_fusion.5
  498.3 0.6 copy-done.4
  499.0 20.5 %custom-call.16 = f32[2,128,128]{1,2,0:T(8,128)S(1)} custom-call(f32[2,128,128]{2,1,0:T(8,128)} %copy-done.4), custom_call_target="InvertDiagBlocksLowerTriangular" | custom-call | tf_op jit(solution)/shard_map/jit(_solve_triangular)/triangular_solve | solution.py:18
  519.4 0.3 fusion.19
  519.8 1.1 convolution_subtract_fusion
  520.9 0.3 fusion.24
  521.2 2.0 convolution_multiply_fusion
  (43 shorter events, 1.1 us)
Async XLA Ops:
  7.2 10.1 %copy-start = (bf16[4096,256]{1,0:T(8,128)(2,1)S(1)}, bf16[4096,256]{1,0:T(8,128)(2,1)}, u32[]{:S(2)}) copy-start(bf16[4096,256]{1,0:T(8,128)(2,1)} %param.9) | copy-start | bytes 6291460
  11.1 45.9 %all-to-all-start = ((s32[8,1,4]{2,1,0:T(1,128)}), s32[8,1,4]{2,1,0:T(1,128)S(1)}, u32[]{:S(2)}, u32[]{:S(2)}) async-start(s32[8,1,4]{2,1,0:T(1,128)} %bitcast.3), calls=%async_computation | async-start | bytes 8192 | tf_op jit(solution)/shard_map/all_to_all | solution.py:48
  57.0 30.8 %all-to-all-start.1 = ((bf16[8,4,128,256]{2,3,1,0:T(8,128)(2,1)}), bf16[8,4,128,256]{2,3,1,0:T(8,128)(2,1)S(1)}, u32[]{:S(2)}, u32[]{:S(2)}) async-start(bf16[8,4,128,256]{2,3,1,0:T(8,128)(2,1)} %broadcast_select_fusion), calls=%async_computation.1 | async-start | bytes 4194304 | tf_op jit(solution)/shard_map/all_to_all | solution.py:47
  61.2 112.8 %reduce-scatter.2.cloned.1.call-start = ((), (), s32[]{:S(2)}) async-start(), calls=%async_computation.3 | async-start | bytes 5242880 | tf_op jit(solution)/shard_map/reduce_scatter | solution.py:57
  87.8 1.4 copy-start.3
  97.6 209.6 %all-reduce.3.cloned.1.call-start = ((), (), s32[]{:S(2)}) async-start(), calls=%async_computation.4 | async-start | bytes 524288 | tf_op jit(solution)/shard_map/psum | solution.py:60
  178.1 271.8 %all-gather.3.cloned.1.call-start = ((), (), s32[]{:S(2)}) async-start(), calls=%async_computation.5 | async-start | bytes 8650752 | tf_op jit(solution)/shard_map/all_gather | solution.py:63
  309.3 60.7 %copy-start.2 = (f32[1024,256]{1,0:T(8,128)S(1)}, f32[1024,256]{1,0:T(8,128)}, u32[]{:S(2)}) copy-start(f32[1024,256]{1,0:T(8,128)} %reduce-scatter.2.cloned.1.call-done) | copy-start | bytes 3145732
  492.5 30.7 %copy-start.1 = (bf16[4096,256]{1,0:T(8,128)(2,1)S(1)}, bf16[4096,256]{1,0:T(8,128)(2,1)}, u32[]{:S(2)}) copy-start(bf16[4096,256]{1,0:T(8,128)(2,1)} %param.9) | copy-start | bytes 6291460
  498.3 0.6 copy-start.4
Sparse Core Ops, SparseCore 0:
  97.8 76.1 reduce-scatter.1
  180.1 127.0 all-reduce.2
  373.7 76.1 all-gather.2
